TPU v7x, 512 devices: a whole 4x8x8 slice. The times are simulated.
512 devices in a mesh: band: 8 (over x, z_lo), tm: 64 (over y, z_hi, core).
Axes of the slice: x: 4, y: 8, z: 8 (z_hi: 4, z_lo: 2; z = z_hi * 2 + z_lo), core: 2. Of those that a mesh axis runs over, the one named last changes fastest.
Arguments:
- driven_wave: bfloat16 [2048, 2048], P('tm', 'band'), may hold values from -6 to 6
- responses: bfloat16 [1024, 512, 2048], P('tm', None, 'band'), may hold values from -0.01171875 to 0.01171875
- tap_counts: int32 [2048], P('band'), may hold values from 256 to 1024
- panel_links: int32 [2048, 2], P('band'), may hold values 0 or 1
Outputs:
- far_end: bfloat16 [1024, 2048], P('tm', 'band')
All inputs are finite; a program needn't handle non-finite values. No bound on the sum of `panel_links` on one device may be relied on, other than what follows from the above.
Results may differ from a plain program's by a relative error of at most 0.00155.
Values may be sent and summed in bfloat16 or wider, within the bound.
No kernel may reach another device: no remote copies, remote signals or barrier semaphores. Data moves between devices by JAX's collectives and lax.ppermute only.
A program may use at most 64 MiB of HBM per device.

v0:
```python
import jax
import jax.numpy as jnp
from jax import lax
from jax.sharding import PartitionSpec as P

SAMP_DEV = 16


def extended(cells, sides, width):
    for axis, dim in sides:
        count = lax.axis_size(axis)
        ends = count - 1
        head = lax.slice_in_dim(cells, 0, width, axis=dim)
        tail = lax.slice_in_dim(cells, cells.shape[dim] - width, cells.shape[dim], axis=dim)
        cells = jnp.concatenate(
            [
                lax.ppermute(tail, axis, [(i, (i + 1) % count) for i in range(ends)]),
                cells,
                lax.ppermute(head, axis, [((i + 1) % count, i) for i in range(ends)]),
            ],
            axis=dim,
        )
    return cells


def masked_weights(responses, tap_counts, panel_links, first_tap):
    tap_dev, coupled_ports, group_ports = responses.shape
    half_width = (coupled_ports - group_ports) // 2
    tap_index = first_tap + jnp.arange(tap_dev, dtype=jnp.int32)
    tap_alive = tap_index[:, None] < tap_counts[None, :]
    port_index = jnp.arange(coupled_ports, dtype=jnp.int32)[:, None]
    lower_open = panel_links[None, :, 0] == 1
    upper_open = panel_links[None, :, 1] == 1
    couple_open = jnp.where(
        port_index < half_width,
        lower_open,
        jnp.where(port_index >= half_width + group_ports, upper_open, True),
    )
    keep_mask = tap_alive[:, None, :] & couple_open[None, :, :]
    return jnp.where(keep_mask, responses, jnp.zeros_like(responses))


def per_device(driven_wave, responses, tap_counts, panel_links):
    tap_dev = responses.shape[0]
    group_ports = driven_wave.shape[1]
    coupled_ports = 2 * group_ports
    half_width = group_ports // 2
    total_taps = tap_dev * lax.axis_size("tm")
    first_tap = lax.axis_index("tm") * tap_dev
    weights = masked_weights(responses, tap_counts, panel_links, first_tap)
    widened = extended(driven_wave, (("band", 1),), half_width)
    history = lax.all_gather(widened, "tm", axis=0, tiled=True)
    block_count = tap_dev // 8
    first_row = jnp.int32(0)

    def add_block(block_index, running):
        lead_tap = (8 * block_index).astype(jnp.int32)
        offset = first_row + total_taps - first_tap - lead_tap - 7
        window = lax.dynamic_slice_in_dim(history, offset, lax.axis_size("tm") * SAMP_DEV + 7, 0)
        stacked = jnp.concatenate(
            [
                window[7 - shift_index : 7 - shift_index + lax.axis_size("tm") * SAMP_DEV]
                for shift_index in range(8)
            ],
            axis=1,
        )
        tap_panel = lax.dynamic_slice_in_dim(weights, lead_tap, 8, 0).reshape(
            8 * coupled_ports, group_ports
        )
        return running + jnp.dot(stacked, tap_panel, preferred_element_type=jnp.float32)

    summed = lax.psum_scatter(
        lax.fori_loop(
            0,
            block_count,
            add_block,
            jnp.zeros((lax.axis_size("tm") * SAMP_DEV, group_ports), jnp.float32),
        ),
        "tm",
        scatter_dimension=0,
        tiled=True,
    )
    return summed.astype(jnp.bfloat16)


def solution(mesh):
    return jax.shard_map(
        per_device,
        mesh=mesh,
        in_specs=(P("tm", "band"), P("tm", None, "band"), P("band"), P("band", None)),
        out_specs=P("tm", "band"),
        check_vma=False,
    )
```

profile of v0, /device:TPU:2, one launch (start us, length us, event | category | flops | bytes accessed | tf_op | source)
XLA Modules:
  0.0 309.9 jit_solution(17289685736764098820)
XLA Ops:
  7.3 4.3 %collective-permute-start = (bf16[32,128]{1,0:T(8,128)(2,1)S(1)}, bf16[32,128]{1,0:T(8,128)(2,1)S(1)}, u32[]{:S(2)}, u32[]{:S(2)}) collective-permute-start(bf16[32,128]{1,0:T(8,128)(2,1)S(1)} %get-tuple-element.208), channel_id=1, source_target_pairs={{0,64},{64,128},{128,192},{192,256},{256,320},{320,384},{384,448},... | collective-permute-start | bytes 24584 | tf_op jit(solution)/shard_map/ppermute | solution.py:17
  11.5 2.5 collective-permute-start.1
  14.0 3.1 collective-permute-done.1
  17.1 1.3 pad_maximum_fusion
  20.3 5.4 %and_select_fusion = bf16[16,512,256]{2,1,0:T(8,128)(2,1)} fusion(bf16[16,512,256]{2,1,0:T(8,128)(2,1)} %param.7, pred[512,256]{1,0:T(8,128)(4,1)S(1)} %select_select_fusion, pred[16,256]{1,0:T(8,128)(4,1)S(1)} %broadcast_compare_fusion), kind=kLoop, calls=%fused_computation.10 | loop fusion | flops 4194304 | bytes 8523776 | tf_op jit(solution)/shard_map/jit(_where)/select_n | solution.py:40
  25.7 82.2 %all-gather.2.cloned.1.call-done = bf16[2048,512]{1,0:T(8,128)(2,1)} async-done(((bf16[32,512]{1,0:T(8,128)(2,1)}), bf16[2048,512]{1,0:T(8,128)(2,1)}) %all-gather.2.cloned.1.call-update) | async-done | bytes 2097168 | tf_op jit(solution)/shard_map/all_gather | solution.py:52
  107.8 46.4 %while.18 = (s32[]{:T(128)}, f32[1024,256]{1,0:T(8,128)S(1)}, s32[]{:T(128)}, bf16[2048,512]{1,0:T(8,128)(2,1)}, bf16[16,512,256]{2,1,0:T(8,128)(2,1)}, /*index=...) while((s32[]{:T(128)}, f32[1024,256]{1,0:T(8,128)S(1)}, ...), condition=%wide.region_1.2_spmd.clone, body=%wide.region_0.1_spmd.clone.sunk | while | flops 2148007936 | bytes 41943464 | solution.py:73
  107.8 2.5 dynamic-slice_dynamic-update-slice_fusion.16
  110.3 2.5 dynamic-slice_dynamic-update-slice_fusion.17
  112.8 2.5 dynamic-slice_dynamic-update-slice_fusion.18
  115.4 2.5 dynamic-slice_dynamic-update-slice_fusion.19
  117.9 1.3 dynamic-slice_dynamic-update-slice_fusion.20
  121.8 1.3 dynamic-slice_dynamic-update-slice_fusion.23
  123.2 1.7 constant_dynamic-slice_fusion.2
  124.9 6.1 %convolution_add_fusion.2 = f32[1024,256]{1,0:T(8,128)S(1)} fusion(bf16[1024,4096]{1,0:T(8,128)(2,1)} %dynamic-slice_dynamic-update-slice_fusion.23, bf16[4096,256]{1,0:T(8,128)(2,1)S(1)} %bitcast.9, f32[1024,256]{1,0:T(8,128)S(1)} %get-tuple-element.262, pred[]{:T(512)S(6)} %compare.3), kind=kOutput, calls=%fused_computation.clone.1 | convolution fusion | flops 2148007936 | bytes 12582913 | tf_op jit(solution)/shard_map/while/body/eval_jaxpr/dot_general | solution.py:70
  131.0 2.5 dynamic-slice_dynamic-update-slice_fusion.16
  133.6 2.5 dynamic-slice_dynamic-update-slice_fusion.17
  136.0 2.5 dynamic-slice_dynamic-update-slice_fusion.18
  138.6 2.5 dynamic-slice_dynamic-update-slice_fusion.19
  141.1 1.3 dynamic-slice_dynamic-update-slice_fusion.20
  145.0 1.3 dynamic-slice_dynamic-update-slice_fusion.23
  146.4 1.7 constant_dynamic-slice_fusion.2
  148.1 6.1 %convolution_add_fusion.2 = f32[1024,256]{1,0:T(8,128)S(1)} fusion(bf16[1024,4096]{1,0:T(8,128)(2,1)} %dynamic-slice_dynamic-update-slice_fusion.23, bf16[4096,256]{1,0:T(8,128)(2,1)S(1)} %bitcast.9, f32[1024,256]{1,0:T(8,128)S(1)} %get-tuple-element.262, pred[]{:T(512)S(6)} %compare.3), kind=kOutput, calls=%fused_computation.clone.1 | convolution fusion | flops 2148007936 | bytes 12582913 | tf_op jit(solution)/shard_map/while/body/eval_jaxpr/dot_general | solution.py:70
  155.2 146.5 %reduce-scatter.2.cloned.1.call-done = f32[16,256]{1,0:T(8,128)} async-done(((f32[1024,256]{1,0:T(8,128)}), f32[16,256]{1,0:T(8,128)}) %reduce-scatter.2.cloned.1.call-update) | async-done | bytes 16400 | tf_op jit(solution)/shard_map/reduce_scatter | solution.py:72
  (23 shorter events, 10.0 us)
Async XLA Ops:
  6.5 101.3 %all-gather.2.cloned.1.call-start = ((), (), s32[]{:S(2)}) async-start(), calls=%async_computation.1 | async-start | bytes 2129920 | tf_op jit(solution)/shard_map/all_gather | solution.py:52
  7.3 6.7 %collective-permute-start = (bf16[32,128]{1,0:T(8,128)(2,1)S(1)}, bf16[32,128]{1,0:T(8,128)(2,1)S(1)}, u32[]{:S(2)}, u32[]{:S(2)}) collective-permute-start(bf16[32,128]{1,0:T(8,128)(2,1)S(1)} %get-tuple-element.208), channel_id=1, source_target_pairs={{0,64},{64,128},{128,192},{192,256},{256,320},{320,384},{384,448},... | collective-permute-start | bytes 24584 | tf_op jit(solution)/shard_map/ppermute | solution.py:17
  11.5 5.5 %collective-permute-start.1 = (bf16[32,128]{1,0:T(8,128)(2,1)S(1)}, bf16[32,128]{1,0:T(8,128)(2,1)S(1)}, u32[]{:S(2)}, u32[]{:S(2)}) collective-permute-start(bf16[32,128]{1,0:T(8,128)(2,1)S(1)} %get-tuple-element.209), channel_id=1, source_target_pairs={{64,0},{128,64},{192,128},{256,192},{320,256},{384,320},{448,384},... | collective-permute-start | bytes 24584 | tf_op jit(solution)/shard_map/ppermute | solution.py:19
  18.4 283.3 %reduce-scatter.2.cloned.1.call-start = ((), (), s32[]{:S(2)}) async-start(), calls=%async_computation.2 | async-start | bytes 1064960 | tf_op jit(solution)/shard_map/reduce_scatter | solution.py:72
  107.8 10.1 %copy-start = (bf16[2048,512]{1,0:T(8,128)(2,1)S(1)}, bf16[2048,512]{1,0:T(8,128)(2,1)}, u32[]{:S(2)}) copy-start(bf16[2048,512]{1,0:T(8,128)(2,1)} %get-tuple-element.282) | copy-start | bytes 6291460 | tf_op jit(solution)/shard_map/while
  131.0 10.1 %copy-start = (bf16[2048,512]{1,0:T(8,128)(2,1)S(1)}, bf16[2048,512]{1,0:T(8,128)(2,1)}, u32[]{:S(2)}) copy-start(bf16[2048,512]{1,0:T(8,128)(2,1)} %get-tuple-element.282) | copy-start | bytes 6291460 | tf_op jit(solution)/shard_map/while
  154.2 1.0 copy-start.1
Sparse Core Ops, SparseCore 0:
  18.5 89.2 all-gather.1
  155.3 146.3 reduce-scatter.1
where the time goes:
time: 311 us; the launch traced here: 310 us
  waiting for transfers between devices  232 us (75%)
  local copies, waits for them, and re-layouts  35.8 us (12%)
  between operations  13.5 us (4%)
  matrix products  12.2 us (4%)
  other arithmetic  9.8 us (3%)
  starting transfers between devices  6.77 us (2%)
    reduce_scatter x1, waiting for transfers between devices, per_device(): lax.psum_scatter(lax.fori_loop(0, block_count, add_block, jnp.zeros((lax....  147 us
    all_gather x1, waiting for transfers between devices, per_device(): history = lax.all_gather(widened, 'tm', axis=0, tiled=True)  82.2 us
    while x18, local copies, waits for them, and re-layouts  28 us
    dot_general x2, matrix products, add_block(): jnp.dot(stacked, tap_panel, preferred_element_type=jnp.float32)  12.2 us
  transfers between devices with their start and end apart: 4, of which 3 were waited for; matrix products, arithmetic and copies ran while one was open for 2% of the time, Pallas kernels for 0%

commit v1 on v0

--- a/solution.py
+++ b/solution.py
@@ -4,6 +4,13 @@
 from jax.sharding import PartitionSpec as P
 
 SAMP_DEV = 16
+
+
+def exchange_gather(shard, mesh_axis, dim):
+    size = lax.axis_size(mesh_axis)
+    blocks = jnp.stack([shard for _ in range(size)])
+    blocks = lax.all_to_all(blocks, mesh_axis, split_axis=0, concat_axis=0)
+    return jnp.concatenate(blocks, axis=dim)
 
 
 def extended(cells, sides, width):
@@ -49,7 +56,7 @@
     first_tap = lax.axis_index("tm") * tap_dev
     weights = masked_weights(responses, tap_counts, panel_links, first_tap)
     widened = extended(driven_wave, (("band", 1),), half_width)
-    history = lax.all_gather(widened, "tm", axis=0, tiled=True)
+    history = exchange_gather(widened, "tm", 0)
     block_count = tap_dev // 8
     first_row = jnp.int32(0)
 

time: 311 us -> 286 us (0.920)
  waiting for transfers between devices: 232 us -> 197 us
  starting transfers between devices: 6.77 us -> 22.4 us
  local copies, waits for them, and re-layouts: 35.8 us -> 29.9 us
    all_gather x1 -> x0, waiting for transfers between devices: 82.2 us -> none  [per_device(): history = lax.all_gather(widened, 'tm', axis=0, tiled=True)]
    all_to_all x0 -> x1, waiting for transfers between devices: none -> 44.8 us  [exchange_gather(): blocks = lax.all_to_all(blocks, mesh_axis, split_axis=0, concat_axis=0)]
    all_to_all x0 -> x1, starting transfers between devices: none -> 15.7 us  [exchange_gather(): blocks = lax.all_to_all(blocks, mesh_axis, split_axis=0, concat_axis=0)]
    while x18 -> x14, local copies, waits for them, and re-layouts: 28 us -> 18 us
where the time goes in v1:
time: 286 us
  waiting for transfers between devices  197 us (69%)
  local copies, waits for them, and re-layouts  29.9 us (10%)
  starting transfers between devices  22.4 us (8%)
  between operations  13.5 us (5%)
  matrix products  13.4 us (5%)
  other arithmetic  9.19 us (3%)
    reduce_scatter x1, waiting for transfers between devices, per_device(): lax.psum_scatter(lax.fori_loop(0, block_count, add_block, jnp.zeros((lax....  150 us
    all_to_all x1, waiting for transfers between devices, exchange_gather(): blocks = lax.all_to_all(blocks, mesh_axis, split_axis=0, concat_axis=0)  44.8 us
    while x14, local copies, waits for them, and re-layouts  18 us
    all_to_all x1, starting transfers between devices, exchange_gather(): blocks = lax.all_to_all(blocks, mesh_axis, split_axis=0, concat_axis=0)  15.7 us
    dot_general x2, matrix products, add_block(): jnp.dot(stacked, tap_panel, preferred_element_type=jnp.float32)  13.4 us
    dynamic_slice x2, local copies, waits for them, and re-layouts, add_block(): lax.dynamic_slice_in_dim(weights, lead_tap, 8, 0)  6.1 us
  transfers between devices with their start and end apart: 4, of which 3 were waited for; matrix products, arithmetic and copies ran while one was open for 2% of the time, Pallas kernels for 0%

profile of v1, /device:TPU:2, one launch (start us, length us, event | category | flops | bytes accessed | tf_op | source)
XLA Modules:
  0.0 285.9 jit_solution(597283215398536425)
XLA Ops:
  7.3 4.3 %collective-permute-start = (bf16[32,128]{1,0:T(8,128)(2,1)S(1)}, bf16[32,128]{1,0:T(8,128)(2,1)S(1)}, u32[]{:S(2)}, u32[]{:S(2)}) collective-permute-start(bf16[32,128]{1,0:T(8,128)(2,1)S(1)} %get-tuple-element.208), channel_id=1, source_target_pairs={{0,64},{64,128},{128,192},{192,256},{256,320},{320,384},{384,448},... | collective-permute-start | bytes 24584 | tf_op jit(solution)/shard_map/ppermute | solution.py:24
  11.5 2.5 collective-permute-start.1
  14.0 3.1 %collective-permute-done.1 = bf16[32,128]{1,0:T(8,128)(2,1)S(1)} collective-permute-done((bf16[32,128]{1,0:T(8,128)(2,1)S(1)}, bf16[32,128]{1,0:T(8,128)(2,1)S(1)}, u32[]{:S(2)}, u32[]{:S(2)}) %collective-permute-start.1) | collective-permute-done | bytes 8224 | tf_op jit(solution)/shard_map/ppermute | solution.py:26
  17.8 1.6 stack.2
  19.4 15.7 %all-to-all-start = ((bf16[64,32,512]{2,1,0:T(8,128)(2,1)}), bf16[64,32,512]{2,1,0:T(8,128)(2,1)S(1)}, u32[]{:S(2)}, u32[]{:S(2)}) async-start(bf16[64,32,512]{2,1,0:T(8,128)(2,1)} %stack.2), calls=%async_computation | async-start | bytes 4194304 | tf_op jit(solution)/shard_map/all_to_all | solution.py:12
  36.9 5.4 %and_select_fusion = bf16[16,512,256]{2,1,0:T(8,128)(2,1)} fusion(bf16[16,512,256]{2,1,0:T(8,128)(2,1)} %param.7, pred[512,256]{1,0:T(8,128)(4,1)S(1)} %select_select_fusion, pred[16,256]{1,0:T(8,128)(4,1)S(1)} %broadcast_compare_fusion), kind=kLoop, calls=%fused_computation.10 | loop fusion | flops 4194304 | bytes 8523776 | tf_op jit(solution)/shard_map/jit(_where)/select_n | solution.py:47
  42.3 44.8 %all-to-all-done = bf16[64,32,512]{2,1,0:T(8,128)(2,1)S(1)} async-done(((bf16[64,32,512]{2,1,0:T(8,128)(2,1)}), bf16[64,32,512]{2,1,0:T(8,128)(2,1)S(1)}, u32[]{:S(2)}, u32[]{:S(2)}) %all-to-all-start) | async-done | bytes 2097184 | tf_op jit(solution)/shard_map/all_to_all | solution.py:12
  87.1 40.1 %while.18 = (s32[]{:T(128)}, f32[1024,256]{1,0:T(8,128)S(1)}, s32[]{:T(128)}, bf16[2048,512]{1,0:T(8,128)(2,1)S(1)}, bf16[16,512,256]{2,1,0:T(8,128)(2,1)}, /*in...) while((s32[]{:T(128)}, f32[1024,256]{1,0:T(8,128)S(1)}, ...), condition=%wide.region_1.2_spmd.clone, body=%wide.region_0.1_spmd.clone.sunk | while | flops 2148007936 | bytes 33554828 | solution.py:80
  88.2 1.3 dynamic-slice_dynamic-update-slice_fusion.17
  89.5 1.3 dynamic-slice_dynamic-update-slice_fusion.18
  90.8 1.3 dynamic-slice_dynamic-update-slice_fusion.19
  92.2 1.3 dynamic-slice_dynamic-update-slice_fusion.20
  94.8 1.3 dynamic-slice_dynamic-update-slice_fusion.22
  97.4 3.1 %constant_dynamic-slice_fusion.2 = bf16[8,512,256]{2,1,0:T(8,128)(2,1)} fusion(bf16[16,512,256]{2,1,0:T(8,128)(2,1)} %get-tuple-element.283, s32[]{:T(128)S(6)} %select_n.57), kind=kLoop, calls=%fused_computation.9.clone.1 | loop fusion | bytes 4194308 | tf_op jit(solution)/shard_map/while/body/eval_jaxpr/dynamic_slice | solution.py:74
  100.4 6.7 %convolution_add_fusion.2 = f32[1024,256]{1,0:T(8,128)S(1)} fusion(bf16[1024,4096]{1,0:T(8,128)(2,1)} %dynamic-slice_dynamic-update-slice_fusion.23, bf16[4096,256]{1,0:T(8,128)(2,1)} %bitcast.11, f32[1024,256]{1,0:T(8,128)S(1)} %get-tuple-element.262, pred[]{:T(512)S(6)} %compare.3), kind=kOutput, calls=%fused_computation.clone.1 | convolution fusion | flops 2148007936 | bytes 12582913 | tf_op jit(solution)/shard_map/while/body/eval_jaxpr/dot_general | solution.py:77
  108.3 1.3 dynamic-slice_dynamic-update-slice_fusion.17
  109.6 1.3 dynamic-slice_dynamic-update-slice_fusion.18
  110.9 1.3 dynamic-slice_dynamic-update-slice_fusion.19
  112.3 1.3 dynamic-slice_dynamic-update-slice_fusion.20
  114.8 1.3 dynamic-slice_dynamic-update-slice_fusion.22
  117.4 3.1 %constant_dynamic-slice_fusion.2 = bf16[8,512,256]{2,1,0:T(8,128)(2,1)} fusion(bf16[16,512,256]{2,1,0:T(8,128)(2,1)} %get-tuple-element.283, s32[]{:T(128)S(6)} %select_n.57), kind=kLoop, calls=%fused_computation.9.clone.1 | loop fusion | bytes 4194308 | tf_op jit(solution)/shard_map/while/body/eval_jaxpr/dynamic_slice | solution.py:74
  120.5 6.7 %convolution_add_fusion.2 = f32[1024,256]{1,0:T(8,128)S(1)} fusion(bf16[1024,4096]{1,0:T(8,128)(2,1)} %dynamic-slice_dynamic-update-slice_fusion.23, bf16[4096,256]{1,0:T(8,128)(2,1)} %bitcast.11, f32[1024,256]{1,0:T(8,128)S(1)} %get-tuple-element.262, pred[]{:T(512)S(6)} %compare.3), kind=kOutput, calls=%fused_computation.clone.1 | convolution fusion | flops 2148007936 | bytes 12582913 | tf_op jit(solution)/shard_map/while/body/eval_jaxpr/dot_general | solution.py:77
  128.2 149.5 %reduce-scatter.2.cloned.1.call-done = f32[16,256]{1,0:T(8,128)} async-done(((f32[1024,256]{1,0:T(8,128)}), f32[16,256]{1,0:T(8,128)}) %reduce-scatter.2.cloned.1.call-update) | async-done | bytes 16400 | tf_op jit(solution)/shard_map/reduce_scatter | solution.py:79
  277.7 1.3 convert_element_type.3
  (19 shorter events, 11.6 us)
Async XLA Ops:
  7.3 6.7 %collective-permute-start = (bf16[32,128]{1,0:T(8,128)(2,1)S(1)}, bf16[32,128]{1,0:T(8,128)(2,1)S(1)}, u32[]{:S(2)}, u32[]{:S(2)}) collective-permute-start(bf16[32,128]{1,0:T(8,128)(2,1)S(1)} %get-tuple-element.208), channel_id=1, source_target_pairs={{0,64},{64,128},{128,192},{192,256},{256,320},{320,384},{384,448},... | collective-permute-start | bytes 24584 | tf_op jit(solution)/shard_map/ppermute | solution.py:24
  11.5 5.5 %collective-permute-start.1 = (bf16[32,128]{1,0:T(8,128)(2,1)S(1)}, bf16[32,128]{1,0:T(8,128)(2,1)S(1)}, u32[]{:S(2)}, u32[]{:S(2)}) collective-permute-start(bf16[32,128]{1,0:T(8,128)(2,1)S(1)} %get-tuple-element.209), channel_id=1, source_target_pairs={{64,0},{128,64},{192,128},{256,192},{320,256},{384,320},{448,384},... | collective-permute-start | bytes 24584 | tf_op jit(solution)/shard_map/ppermute | solution.py:26
  19.4 67.7 %all-to-all-start = ((bf16[64,32,512]{2,1,0:T(8,128)(2,1)}), bf16[64,32,512]{2,1,0:T(8,128)(2,1)S(1)}, u32[]{:S(2)}, u32[]{:S(2)}) async-start(bf16[64,32,512]{2,1,0:T(8,128)(2,1)} %stack.2), calls=%async_computation | async-start | bytes 4194304 | tf_op jit(solution)/shard_map/all_to_all | solution.py:12
  35.1 242.7 %reduce-scatter.2.cloned.1.call-start = ((), (), s32[]{:S(2)}) async-start(), calls=%async_computation.2 | async-start | bytes 1064960 | tf_op jit(solution)/shard_map/reduce_scatter | solution.py:79
  127.2 1.0 copy-start
Sparse Core Ops, SparseCore 0:
  128.3 149.3 reduce-scatter.1
